TPU v7x, 32 devices: a whole 2x2x4 slice. The times are simulated.
32 devices in a mesh: gx: 8 (over z, x), gy: 2 (over y), pa: 2 (over core).
Axes of the slice: x: 2, y: 2, z: 4, core: 2. Of those that a mesh axis runs over, the one named last changes fastest.
Arguments:
- leaf_maps: bfloat16 [8, 2, 2, 1024, 1024], P('gx', 'gy', None, 'pa'), may hold values from -0.125 to 0.125
- face_index: int32 [8, 2, 1024], P('gx', 'gy'), may hold values from 0 to 1023, each once within a row
- order_x: int32 [4, 2], replicated, may hold values from 0 to 1
- order_y: int32 [4, 1], replicated, may hold values from 0 to 1
- traces: float32 [8, 2, 2, 1024], P('gx', 'gy'), may hold values from -6 to 6
Outputs:
- merged_map: bfloat16 [8, 2, 2, 2, 128, 1024], P('gx', 'gy', 'pa')
- outgoing: float32 [8, 2, 2, 2, 128], P('gx', 'gy', 'pa')
Inputs may be any that keep to these rules, and one draw needn't show every extreme that they name: `face_index`: each row is a permutation of 0 to 1023.
All inputs are finite; a program needn't handle non-finite values.
Results may differ from a plain program's by a relative error of at most 0.0058.
Values may be sent and summed in bfloat16 or wider, within the bound.
A program may use at most 64 MiB of HBM per device.

v0:
```python
import jax
import jax.numpy as jnp
from jax import lax
from jax.experimental import pallas as pl
from jax.experimental.pallas import tpu as pltpu
from jax.sharding import PartitionSpec as P

MESH = pl.DeviceIdType.MESH
CHUNKS = 8
TILE = 256


def kernel(
    order_x_ref, order_y_ref, leaf_ref, index_ref, trace_ref, map_ref, out_ref,
    held, raw, index_own, pick, trace_all, work, ask, ask_in, reply, reply_in,
    total, local_sem,
    xs, xr, ys, yr, ps, pr, ss, sr, ts, tr,
):
    gx, gy, pa = lax.axis_index("gx"), lax.axis_index("gy"), lax.axis_index("pa")
    half, vert = gx % 2, gy % 2
    xpeer = {"gx": gx + 1 - 2 * half}
    ypeer = {"gy": gy + 1 - 2 * vert}
    dpeer = {"gx": gx + 1 - 2 * half, "gy": gy + 1 - 2 * vert}
    cpeer = {"pa": 1 - pa}
    panel, width = leaf_ref.shape[1], leaf_ref.shape[2]
    step = panel // CHUNKS
    rows = map_ref.shape[1]

    barrier = pltpu.get_barrier_semaphore()
    for peer in (xpeer, ypeer, dpeer, cpeer):
        pl.semaphore_signal(barrier, inc=1, device_id=peer, device_id_type=MESH)

    load_index = pltpu.make_async_copy(index_ref, index_own, local_sem.at[0])
    load_index.start()
    load_leaf = pltpu.make_async_copy(leaf_ref, raw, local_sem.at[1])
    load_leaf.start()
    load_trace = pltpu.make_async_copy(trace_ref, trace_all.at[0], local_sem.at[2])
    load_trace.start()

    def send(src, dst, ssem, rsem, peer):
        copy = pltpu.make_async_remote_copy(
            src_ref=src, dst_ref=dst, send_sem=ssem, recv_sem=rsem,
            device_id=peer, device_id_type=MESH,
        )
        copy.start()
        return copy

    def part(rel, k):
        return held.at[rel, :, pl.ds(pl.multiple_of(pa * panel + k * step, step), step), :]

    load_index.wait()
    index_row = index_own[...]
    grain = 256
    for n in range(width // grain):
        places = lax.broadcasted_iota(jnp.int32, (grain, width), 0) + n * grain
        pick[n * grain : (n + 1) * grain] = (places == index_row).astype(jnp.float32).astype(jnp.bfloat16)
    load_leaf.wait()

    def permute(k):
        chunk = raw[:, k * step : (k + 1) * step, :].reshape(2 * step, width)
        value = jnp.dot(chunk, pick[...], preferred_element_type=jnp.float32).astype(jnp.bfloat16)
        held[0, :, pl.ds(pl.multiple_of(pa * panel + k * step, step), step), :] = value.reshape(2, step, width)

    xcopy, ycopy = {}, {}

    def send_both(k):
        xcopy[k] = send(part(0, k), part(1, k), xs.at[k], xr.at[k], xpeer)
        ycopy[k] = send(part(0, k), part(2, k), ys.at[k], yr.at[k], ypeer)

    permute(0)
    permute(1)
    pl.semaphore_wait(barrier, 4)
    for k in range(2, CHUNKS):
        send_both(k - 2)
        permute(k)
    send_both(CHUNKS - 2)
    send_both(CHUNKS - 1)
    own = held.at[0, :, pl.ds(pl.multiple_of(pa * panel, panel), panel), :]
    shared = [send(own, own, ps.at[0, 0], pr.at[0, 0], cpeer)]
    small = []
    for n, peer in ((1, xpeer), (2, ypeer), (3, dpeer)):
        small.append(send(trace_ref, trace_all.at[n], ss.at[n], sr.at[n], peer))

    def share(rel, k):
        shared.append(send(part(rel, k), part(rel, k), ps.at[rel, k], pr.at[rel, k], cpeer))

    for k in range(CHUNKS):
        xcopy[k].wait_recv()
        share(1, k)
        ycopy[k].wait_recv()
        share(2, k)
    load_trace.wait()
    for copy in small + shared:
        copy.wait_recv()

    pair, base = gx // 2, gy - vert
    right2 = order_y_ref[gy // 2, pair]
    left2 = 1 - right2
    bit_left = order_x_ref[base + left2, pair]
    bit_right = order_x_ref[base + right2, pair]

    def slot(h, v):
        return (h + half) % 2 + 2 * ((v + vert) % 2)

    slots = [
        slot(1 - bit_left, left2), slot(bit_left, left2),
        slot(1 - bit_right, right2), slot(bit_right, right2),
    ]
    here = [jnp.minimum(which, 2) for which in slots]
    first = pl.multiple_of(pa * panel + half * (2 * rows) + vert * rows, rows)

    def times(src, dst, which, use=None, after=None):
        left = src[...].reshape(2 * rows, width)
        for n in range(width // TILE):
            cols = slice(n * TILE, (n + 1) * TILE)
            by = [jnp.dot(left, held[which, c, :, cols], preferred_element_type=jnp.float32) for c in range(2)]
            real = (by[0][:rows] - by[1][rows:]).astype(jnp.bfloat16)
            imag = (by[1][:rows] + by[0][rows:]).astype(jnp.bfloat16)
            if use is not None:
                real = jnp.where(use, real, src[0, :, cols])
                imag = jnp.where(use, imag, src[1, :, cols])
            dst[0, :, cols] = real
            dst[1, :, cols] = imag
            if after is not None and n:
                after(n - 1)
        if after is not None:
            after(width // TILE - 1)

    spot = lax.broadcasted_iota(jnp.int32, (rows, width), 0) + first
    unit = (lax.broadcasted_iota(jnp.int32, (rows, width), 1) == spot).astype(jnp.float32).astype(jnp.bfloat16)
    away = slots[0] == 3
    work[0, 0] = jnp.where(away, unit, held[here[0], 0, pl.ds(first, rows), :])
    work[0, 1] = jnp.where(away, jnp.zeros_like(unit), held[here[0], 1, pl.ds(first, rows), :])
    times(work.at[0], work.at[1], here[1], slots[2] // 3 + slots[3] // 3 > 0)
    peer = {"gx": gx + (1 - 2 * half) * (1 - pa), "gy": gy + (1 - 2 * vert) * pa}
    tiles = width // TILE

    def tile_of(ref, n):
        return ref.at[:, :, n * TILE : (n + 1) * TILE]

    def sender(src, dst, row, copies):
        def after(n):
            copies.append(send(tile_of(src, n), tile_of(dst, n), ts.at[row, n], tr.at[row, n], peer))
        return after

    def times_arriving(copies, src, dst, which, use=None, after=None):
        for n in range(tiles):
            deep = slice(n * TILE, (n + 1) * TILE)
            copies[n].wait_recv()
            left = src[:, :, deep].reshape(2 * rows, TILE)
            for m in range(tiles):
                cols = slice(m * TILE, (m + 1) * TILE)
                by = []
                for c in range(2):
                    term = jnp.dot(left, held[which, c, deep, cols], preferred_element_type=jnp.float32)
                    if n:
                        term += total[c, :, cols]
                    if n < tiles - 1:
                        total[c, :, cols] = term
                    by.append(term)
                if n == tiles - 1:
                    real = (by[0][:rows] - by[1][rows:]).astype(jnp.bfloat16)
                    imag = (by[1][:rows] + by[0][rows:]).astype(jnp.bfloat16)
                    if use is not None:
                        real = jnp.where(use, real, src[0, :, cols])
                        imag = jnp.where(use, imag, src[1, :, cols])
                    dst[0, :, cols] = real
                    dst[1, :, cols] = imag
                    if after is not None and m:
                        after(m - 1)
        if after is not None:
            after(tiles - 1)

    asked, replied = [], []
    times(work.at[1], ask, here[2], slots[3] == 3, sender(ask, ask_in, 0, asked))
    times_arriving(asked, ask_in, reply, 2 - pa, None, sender(reply, reply_in, 1, replied))
    times_arriving(replied, reply_in, work.at[0], here[1], away)
    times(work.at[0], work.at[1], here[2], slots[0] // 3 + slots[1] // 3 > 0)
    times(work.at[1], map_ref, here[3], slots[3] != 3)
    trace = (trace_all[0] + trace_all[1]) + (trace_all[2] + trace_all[3])
    wide = map_ref[...].reshape(2 * rows, width).astype(jnp.float32)
    ones = jnp.ones((8, 128), jnp.float32)
    dims = (((1,), (1,)), ((), ()))
    sums = []
    for c in range(2):
        scaled = wide * trace[c : c + 1]
        folded = scaled[:, :128]
        for n in range(1, width // 128):
            folded += scaled[:, n * 128 : (n + 1) * 128]
        sums.append(lax.dot_general(ones, folded, dims, precision=lax.Precision.HIGHEST, preferred_element_type=jnp.float32))
    out_ref[0:1] = sums[0][0:1, :rows] - sums[1][0:1, rows:]
    out_ref[1:2] = sums[1][0:1, :rows] + sums[0][0:1, rows:]

    for copy in small + list(xcopy.values()) + list(ycopy.values()) + shared + asked + replied:
        copy.wait_send()


def per_device(leaf_maps, face_index, order_x, order_y, traces):
    leaf = leaf_maps[0, 0]
    _, panel, width = leaf.shape
    rows = panel // 4
    vmem = pl.BlockSpec(memory_space=pltpu.VMEM)
    smem = pl.BlockSpec(memory_space=pltpu.SMEM)
    hbm = pl.BlockSpec(memory_space=pl.ANY)
    dma = pltpu.SemaphoreType.DMA
    merged, outgoing = pl.pallas_call(
        kernel,
        out_shape=(
            pltpu.VMEM((2, rows, width), jnp.bfloat16),
            pltpu.VMEM((2, rows), jnp.float32),
        ),
        in_specs=[smem, smem, hbm, hbm, hbm],
        out_specs=(vmem, vmem),
        scratch_shapes=[
            pltpu.VMEM((3, 2, 2 * panel, width), jnp.bfloat16),
            pltpu.VMEM((2, panel, width), jnp.bfloat16),
            pltpu.VMEM((1, width), jnp.int32),
            pltpu.VMEM((width, width), jnp.bfloat16),
            pltpu.VMEM((4, 2, width), jnp.float32),
            pltpu.VMEM((2, 2, rows, width), jnp.bfloat16),
            pltpu.VMEM((2, rows, width), jnp.bfloat16),
            pltpu.VMEM((2, rows, width), jnp.bfloat16),
            pltpu.VMEM((2, rows, width), jnp.bfloat16),
            pltpu.VMEM((2, rows, width), jnp.bfloat16),
            pltpu.VMEM((2, 2 * rows, width), jnp.float32),
            dma((3,)),
            dma((CHUNKS,)), dma((CHUNKS,)),
            dma((CHUNKS,)), dma((CHUNKS,)),
            dma((3, CHUNKS)), dma((3, CHUNKS)),
            dma((4,)), dma((4,)),
            dma((2, width // TILE)), dma((2, width // TILE)),
        ],
        compiler_params=pltpu.CompilerParams(
            collective_id=0, has_side_effects=True, vmem_limit_bytes=60 * 1024 * 1024
        ),
    )(order_x.T, order_y.T, leaf, face_index[0], traces[0, 0])
    return (
        merged.reshape(1, 1, 1, 2, rows, width),
        outgoing.reshape(1, 1, 1, 2, rows),
    )


def solution(mesh):
    placed = (
        P("gx", "gy", None, "pa", None),
        P("gx", "gy", None),
        P(),
        P(),
        P("gx", "gy", None, None),
    )
    return jax.shard_map(
        per_device,
        mesh=mesh,
        in_specs=placed,
        out_specs=(P("gx", "gy", "pa", None, None, None), P("gx", "gy", "pa", None, None)),
        check_vma=False,
    )
```

profile of v0, /device:TPU:0, one launch (start us, length us, event | category | flops | bytes accessed | tf_op | source)
XLA Modules:
  0.0 77.5 jit_solution(1207282153756824533)
XLA Ops:
  0.6 75.5 %shard_map.68 = (bf16[2,128,1024]{2,1,0:T(8,128)(2,1)S(1)}, f32[2,128]{1,0:T(2,128)S(1)}) custom-call(s32[2,4]{1,0:T(2,128)} %bitcast.12, s32[1,4]{1,0:T(1,128)} %bitcast.13, bf16[2,512,1024]{2,1,0:T(8,128)(2,1)} %bitcast.9, s32[1,1024]{1,0:T(1,128)} %bitcast.11, f32[2,1024]{1,0:T(2,128)} %bitcast.10), custom_call_target="tpu_custom_call" | custom-call | tf_op jit(solution)/shard_map/pallas_call | solution.py:206
  76.1 0.8 %copy.9 = bf16[1,1,1,2,128,1024]{5,4,3,2,1,0:T(8,128)(2,1)} copy(bf16[1,1,1,2,128,1024]{5,4,3,2,1,0:T(8,128)(2,1)S(1)} %bitcast.7) | data formatting | bytes 1048576
  76.9 0.6 copy.10
where the time goes:
time: 77.7 us; the launch traced here: 77.5 us
  Pallas kernels  75.5 us (97%)
  local copies, waits for them, and re-layouts  1.36 us (2%)
    pallas_call x1, Pallas kernels, per_device(): pl.pallas_call(kernel, out_shape=(pltpu.VMEM((2, rows, width), jnp.bfloat...  75.5 us

commit v1 on v0

v1 whole, which is shorter than its diff:
```python
import jax
import jax.numpy as jnp
from jax import lax
from jax.experimental import pallas as pl
from jax.experimental.pallas import tpu as pltpu
from jax.sharding import PartitionSpec as P

MESH = pl.DeviceIdType.MESH
STEPS = 16
LEAD = 2
LAG = 2
BLOCKS = 4
TILE = 256
NT = (((1,), (1,)), ((), ()))


def hot(flags):
    return flags.astype(jnp.float32).astype(jnp.bfloat16)


def mul(left, right):
    return jnp.dot(left, right, preferred_element_type=jnp.float32)


def mul_t(left, right):
    return lax.dot_general(left, right, NT, preferred_element_type=jnp.float32)


def kernel(
    order_x_ref, order_y_ref, leaf_ref, index_ref, trace_ref, map_ref, out_ref,
    raw, index_own, pick, own, outbox, inbox, prod, trace_all, local_sem,
    os, orv, xs, xr, ys, yr, ps, pr, ss, sr,
):
    gx, gy, pa = lax.axis_index("gx"), lax.axis_index("gy"), lax.axis_index("pa")
    half, vert = gx % 2, gy % 2
    other_x, other_y = gx + 1 - 2 * half, gy + 1 - 2 * vert
    ypeer = {"gy": other_y}
    dpeer = {"gx": other_x, "gy": other_y}
    cpeer = {"pa": 1 - pa}
    panel, width = leaf_ref.shape[1], leaf_ref.shape[2]
    rows = map_ref.shape[1]
    quarter = panel // 2
    grain = quarter // STEPS

    barrier = pltpu.get_barrier_semaphore()
    for peer in ({"gx": other_x, "pa": 0}, {"gx": other_x, "pa": 1}, ypeer, dpeer, cpeer):
        pl.semaphore_signal(barrier, inc=1, device_id=peer, device_id_type=MESH)

    load_index = pltpu.make_async_copy(index_ref, index_own, local_sem.at[0])
    load_index.start()
    load_leaf = pltpu.make_async_copy(leaf_ref, raw, local_sem.at[1])
    load_leaf.start()
    load_trace = pltpu.make_async_copy(trace_ref, trace_all.at[0], local_sem.at[2])
    load_trace.start()

    pair, base = gx // 2, gy - vert
    right2 = order_y_ref[gy // 2, pair]
    bit_own = order_x_ref[gy, pair]
    bit_y = order_x_ref[other_y, pair]
    own_left = bit_own != half
    y_left = bit_y != half
    own_second = right2 == vert

    def remote(src, dst, ssem, rsem, peer):
        return pltpu.make_async_remote_copy(
            src_ref=src, dst_ref=dst, send_sem=ssem, recv_sem=rsem,
            device_id=peer, device_id_type=MESH,
        )

    block = panel // BLOCKS

    def own_copy(n):
        part = own.at[:, pa, n * block : (n + 1) * block, :]
        return remote(part, part, os.at[n], orv.at[n], cpeer)

    def x_copy(j, core, source):
        return remote(
            outbox.at[j, core], inbox.at[j, source], xs.at[j, core], xr.at[j, source],
            {"gx": other_x, "pa": core},
        )

    def chunk(slot, j, core):
        start = pl.multiple_of(core * quarter + j * grain, grain)
        return prod.at[slot, :, :, pl.ds(start, grain), :]

    def y_copy(j):
        return remote(chunk(0, j, pa), chunk(1, j, pa), ys.at[j], yr.at[j], ypeer)

    def share(slot, j):
        part = chunk(slot, j, pa)
        return remote(part, part, ps.at[slot, j], pr.at[slot, j], cpeer)

    def trace_copy(n, peer):
        return remote(trace_ref, trace_all.at[n], ss.at[n], sr.at[n], peer)

    traces = [trace_copy(n, peer) for n, peer in ((1, {"gx": other_x}), (2, ypeer), (3, dpeer))]

    load_index.wait()
    index_row = index_own[...]
    for n in range(width // TILE):
        places = lax.broadcasted_iota(jnp.int32, (TILE, width), 0) + n * TILE
        pick[n * TILE : (n + 1) * TILE] = hot(places == index_row)
    load_leaf.wait()

    def permute(n):
        part = raw[:, n * block : (n + 1) * block, :].reshape(2 * block, width)
        value = mul(part, pick[...]).astype(jnp.bfloat16)
        own[:, pa, n * block : (n + 1) * block, :] = value.reshape(2, block, width)

    def stage(j):
        row = lax.broadcasted_iota(jnp.int32, (4 * grain, width), 0)
        core, side, spot = row // (2 * grain), (row // grain) % 2, row % grain
        place = side * panel + core * quarter + j * grain + spot
        unit = hot(lax.broadcasted_iota(jnp.int32, (4 * grain, width), 1) == place)
        for c in range(2):
            turned = mul_t(unit, own[c, pa]).astype(jnp.bfloat16)
            for core in range(2):
                start = pl.multiple_of(core * quarter + j * grain, grain)
                plain = own[c, pa, pl.ds(start, grain), :]
                for side in range(2):
                    at = (2 * core + side) * grain
                    outbox[j, core, c, side * grain : (side + 1) * grain, :] = jnp.where(
                        own_left, plain[:, side * panel : (side + 1) * panel], turned[at : at + grain]
                    )
        for core in range(2):
            x_copy(j, core, pa).start()

    permute(0)
    pl.semaphore_wait(barrier, 5)
    own_copy(0).start()
    for n in range(1, BLOCKS):
        permute(n)
        own_copy(n).start()

    def first(j, carry):
        stage(j)
        return carry

    lax.fori_loop(0, LEAD, first, 0)
    for copy in traces:
        copy.start()
    for n in range(BLOCKS):
        own_copy(n).wait_recv()

    def step(j, carry):
        @pl.when(j < STEPS - LEAD)
        def _():
            stage(j + LEAD)

        for source in range(2):
            x_copy(j, 0, source).wait_recv()
        stack = []
        for c in range(2):
            near = [[inbox[j, b, c, t * grain : (t + 1) * grain, :] for t in range(2)] for b in range(2)]
            stack.append(jnp.concatenate([near[0][0], jnp.where(own_left, near[1][0], near[0][1])], axis=1))
            stack.append(jnp.concatenate([jnp.where(own_left, near[0][1], near[1][0]), near[1][1]], axis=1))
        left = jnp.concatenate(stack, axis=0)
        size = 2 * grain
        start = pl.multiple_of(pa * quarter + j * grain, grain)
        for n in range(width // TILE):
            cols = slice(n * TILE, (n + 1) * TILE)
            here = slice(n * TILE % panel, n * TILE % panel + TILE)
            by = []
            for c in range(2):
                plain = mul(left, own[c, :, :, cols].reshape(width, TILE))
                turned = mul_t(left, own[c, n * TILE // panel, here, :])
                by.append(jnp.where(own_left, turned, plain))
            real = (by[0][:size] - by[1][size:]).astype(jnp.bfloat16)
            imag = (by[1][:size] + by[0][size:]).astype(jnp.bfloat16)
            prod[0, 0, :, pl.ds(start, grain), cols] = real.reshape(2, grain, TILE)
            prod[0, 1, :, pl.ds(start, grain), cols] = imag.reshape(2, grain, TILE)
        y_copy(j).start()
        share(0, j).start()

        @pl.when(j >= LAG)
        def _():
            y_copy(j - LAG).wait_recv()
            share(1, j - LAG).start()

        return carry

    lax.fori_loop(0, STEPS, step, 0)
    for j in range(STEPS - LAG, STEPS):
        y_copy(j).wait_recv()
        share(1, j).start()
    load_trace.wait()
    for copy in traces:
        copy.wait_recv()

    def arrived(j, carry):
        share(0, j).wait_recv()
        share(1, j).wait_recv()
        return carry

    lax.fori_loop(0, STEPS, arrived, 0)

    slot_left = jnp.where(own_second, 1, 0)
    slot_right = 1 - slot_left
    left_turned = jnp.where(own_second, y_left, own_left)
    right_turned = jnp.where(own_second, own_left, y_left)
    within = pl.multiple_of(half * quarter + vert * rows, rows)
    whole = pl.multiple_of(pa * panel + half * quarter + vert * rows, rows)
    unit = hot(
        lax.broadcasted_iota(jnp.int32, (rows, rows), 0) == lax.broadcasted_iota(jnp.int32, (rows, rows), 1)
    )
    stack = []
    for c in range(2):
        plain = prod[slot_left, c, pa, pl.ds(within, rows), :]
        column = prod[slot_left, c, :, :, pl.ds(whole, rows)].reshape(width, rows)
        turned = mul_t(unit, column).astype(jnp.bfloat16)
        stack.append(jnp.where(left_turned, turned, plain))
    left = jnp.concatenate(stack, axis=0)
    for n in range(width // TILE):
        cols = slice(n * TILE, (n + 1) * TILE)
        here = slice(n * TILE % panel, n * TILE % panel + TILE)
        by = []
        for c in range(2):
            plain = mul(left, prod[slot_right, c, :, :, cols].reshape(width, TILE))
            turned = mul_t(left, prod[slot_right, c, n * TILE // panel, here, :])
            by.append(jnp.where(right_turned, turned, plain))
        map_ref[0, :, cols] = (by[0][:rows] - by[1][rows:]).astype(jnp.bfloat16)
        map_ref[1, :, cols] = (by[1][:rows] + by[0][rows:]).astype(jnp.bfloat16)

    trace = (trace_all[0] + trace_all[1]) + (trace_all[2] + trace_all[3])
    wide = map_ref[...].reshape(2 * rows, width).astype(jnp.float32)
    ones = jnp.ones((8, 128), jnp.float32)
    sums = []
    for c in range(2):
        scaled = wide * trace[c : c + 1]
        folded = scaled[:, :128]
        for n in range(1, width // 128):
            folded += scaled[:, n * 128 : (n + 1) * 128]
        sums.append(lax.dot_general(ones, folded, NT, precision=lax.Precision.HIGHEST, preferred_element_type=jnp.float32))
    out_ref[0:1] = sums[0][0:1, :rows] - sums[1][0:1, rows:]
    out_ref[1:2] = sums[1][0:1, :rows] + sums[0][0:1, rows:]

    def sent(j, carry):
        for core in range(2):
            x_copy(j, core, pa).wait_send()
        y_copy(j).wait_send()
        share(0, j).wait_send()
        share(1, j).wait_send()
        return carry

    lax.fori_loop(0, STEPS, sent, 0)
    for n in range(BLOCKS):
        own_copy(n).wait_send()
    for copy in traces:
        copy.wait_send()


def per_device(leaf_maps, face_index, order_x, order_y, traces):
    leaf = leaf_maps[0, 0]
    _, panel, width = leaf.shape
    rows = panel // 4
    grain = panel // 2 // STEPS
    vmem = pl.BlockSpec(memory_space=pltpu.VMEM)
    smem = pl.BlockSpec(memory_space=pltpu.SMEM)
    hbm = pl.BlockSpec(memory_space=pl.ANY)
    dma = pltpu.SemaphoreType.DMA
    merged, outgoing = pl.pallas_call(
        kernel,
        out_shape=(
            pltpu.VMEM((2, rows, width), jnp.bfloat16),
            pltpu.VMEM((2, rows), jnp.float32),
        ),
        in_specs=[smem, smem, hbm, hbm, hbm],
        out_specs=(vmem, vmem),
        scratch_shapes=[
            pltpu.VMEM((2, panel, width), jnp.bfloat16),
            pltpu.VMEM((1, width), jnp.int32),
            pltpu.VMEM((width, width), jnp.bfloat16),
            pltpu.VMEM((2, 2, panel, width), jnp.bfloat16),
            pltpu.VMEM((STEPS, 2, 2, 2 * grain, panel), jnp.bfloat16),
            pltpu.VMEM((STEPS, 2, 2, 2 * grain, panel), jnp.bfloat16),
            pltpu.VMEM((2, 2, 2, panel, width), jnp.bfloat16),
            pltpu.VMEM((4, 2, width), jnp.float32),
            dma((3,)),
            dma((BLOCKS,)), dma((BLOCKS,)),
            dma((STEPS, 2)), dma((STEPS, 2)),
            dma((STEPS,)), dma((STEPS,)),
            dma((2, STEPS)), dma((2, STEPS)),
            dma((4,)), dma((4,)),
        ],
        compiler_params=pltpu.CompilerParams(
            collective_id=0, has_side_effects=True, vmem_limit_bytes=60 * 1024 * 1024
        ),
    )(order_x.T, order_y.T, leaf, face_index[0], traces[0, 0])
    return (
        merged.reshape(1, 1, 1, 2, rows, width),
        outgoing.reshape(1, 1, 1, 2, rows),
    )


def solution(mesh):
    placed = (
        P("gx", "gy", None, "pa", None),
        P("gx", "gy", None),
        P(),
        P(),
        P("gx", "gy", None, None),
    )
    return jax.shard_map(
        per_device,
        mesh=mesh,
        in_specs=placed,
        out_specs=(P("gx", "gy", "pa", None, None, None), P("gx", "gy", "pa", None, None)),
        check_vma=False,
    )
```

time: 77.7 us -> 70.9 us (0.912)
  Pallas kernels: 75.5 us -> 68.7 us
    pallas_call x1, Pallas kernels: 75.5 us -> 68.7 us  [per_device(): pl.pallas_call(kernel, out_shape=(pltpu.VMEM((2, rows, width), jnp.bfloat...]
where the time goes in v1:
time: 70.9 us; the launch traced here: 70.7 us
  Pallas kernels  68.7 us (97%)
  local copies, waits for them, and re-layouts  1.36 us (2%)
    pallas_call x1, Pallas kernels, per_device(): pl.pallas_call(kernel, out_shape=(pltpu.VMEM((2, rows, width), jnp.bfloat...  68.7 us

profile of v1, /device:TPU:0, one launch (start us, length us, event | category | flops | bytes accessed | tf_op | source)
XLA Modules:
  0.0 70.7 jit_solution(3659817548562650749)
XLA Ops:
  0.6 68.7 %shard_map.68 = (bf16[2,128,1024]{2,1,0:T(8,128)(2,1)S(1)}, f32[2,128]{1,0:T(2,128)S(1)}) custom-call(s32[2,4]{1,0:T(2,128)} %bitcast.12, s32[1,4]{1,0:T(1,128)} %bitcast.13, bf16[2,512,1024]{2,1,0:T(8,128)(2,1)} %bitcast.9, s32[1,1024]{1,0:T(1,128)} %bitcast.11, f32[2,1024]{1,0:T(2,128)} %bitcast.10), custom_call_target="tpu_custom_call" | custom-call | tf_op jit(solution)/shard_map/pallas_call | solution.py:261
  69.3 0.8 %copy.9 = bf16[1,1,1,2,128,1024]{5,4,3,2,1,0:T(8,128)(2,1)} copy(bf16[1,1,1,2,128,1024]{5,4,3,2,1,0:T(8,128)(2,1)S(1)} %bitcast.7) | data formatting | bytes 1048576
  70.1 0.6 copy.10

commit v2 on v1

--- a/solution.py
+++ b/solution.py
@@ -7,9 +7,8 @@
 
 MESH = pl.DeviceIdType.MESH
 STEPS = 16
-LEAD = 2
+LEAD = 4
 LAG = 2
-BLOCKS = 4
 TILE = 256
 NT = (((1,), (1,)), ((), ()))
 
@@ -28,7 +27,7 @@
 
 def kernel(
     order_x_ref, order_y_ref, leaf_ref, index_ref, trace_ref, map_ref, out_ref,
-    raw, index_own, pick, own, outbox, inbox, prod, trace_all, local_sem,
+    raw, index_own, pick, plain_own, turned_own, factor, outbox, inbox, prod, trace_all, local_sem,
     os, orv, xs, xr, ys, yr, ps, pr, ss, sr,
 ):
     gx, gy, pa = lax.axis_index("gx"), lax.axis_index("gy"), lax.axis_index("pa")
@@ -67,11 +66,9 @@
             device_id=peer, device_id_type=MESH,
         )
 
-    block = panel // BLOCKS
-
-    def own_copy(n):
-        part = own.at[:, pa, n * block : (n + 1) * block, :]
-        return remote(part, part, os.at[n], orv.at[n], cpeer)
+    def own_copy(n, c):
+        part = factor.at[2 * n + pa, c]
+        return remote(part, part, os.at[n, c], orv.at[n, c], cpeer)
 
     def x_copy(j, core, source):
         return remote(
@@ -83,8 +80,13 @@
         start = pl.multiple_of(core * quarter + j * grain, grain)
         return prod.at[slot, :, :, pl.ds(start, grain), :]
 
-    def y_copy(j):
-        return remote(chunk(0, j, pa), chunk(1, j, pa), ys.at[j], yr.at[j], ypeer)
+    def y_copy(j, n):
+        start = pl.multiple_of(pa * quarter + j * grain, grain)
+        cols = slice(n * panel, (n + 1) * panel)
+        return remote(
+            prod.at[0, :, :, pl.ds(start, grain), cols], prod.at[1, :, :, pl.ds(start, grain), cols],
+            ys.at[j, n], yr.at[j, n], ypeer,
+        )
 
     def share(slot, j):
         part = chunk(slot, j, pa)
@@ -102,35 +104,36 @@
         pick[n * TILE : (n + 1) * TILE] = hot(places == index_row)
     load_leaf.wait()
 
-    def permute(n):
-        part = raw[:, n * block : (n + 1) * block, :].reshape(2 * block, width)
-        value = mul(part, pick[...]).astype(jnp.bfloat16)
-        own[:, pa, n * block : (n + 1) * block, :] = value.reshape(2, block, width)
+    def permute(c):
+        for n in range(width // TILE):
+            cols = slice(n * TILE, (n + 1) * TILE)
+            value = mul(raw[c], pick[:, cols]).astype(jnp.bfloat16)
+            plain_own[c, :, cols] = value
+            turned_own[c, cols, :] = value.T
+        for n, which in ((0, pa), (1, 1 - pa)):
+            place = pl.ds(pl.multiple_of(which * panel, panel), panel)
+            factor[2 * n + pa, c] = jnp.where(own_left, turned_own[c, place, :], plain_own[c, :, place])
 
     def stage(j):
-        row = lax.broadcasted_iota(jnp.int32, (4 * grain, width), 0)
-        core, side, spot = row // (2 * grain), (row // grain) % 2, row % grain
-        place = side * panel + core * quarter + j * grain + spot
-        unit = hot(lax.broadcasted_iota(jnp.int32, (4 * grain, width), 1) == place)
-        for c in range(2):
-            turned = mul_t(unit, own[c, pa]).astype(jnp.bfloat16)
-            for core in range(2):
+        for core in range(2):
+            for side in range(2):
                 start = pl.multiple_of(core * quarter + j * grain, grain)
-                plain = own[c, pa, pl.ds(start, grain), :]
-                for side in range(2):
-                    at = (2 * core + side) * grain
-                    outbox[j, core, c, side * grain : (side + 1) * grain, :] = jnp.where(
-                        own_left, plain[:, side * panel : (side + 1) * panel], turned[at : at + grain]
-                    )
+                deep = pl.multiple_of(side * panel + core * quarter + j * grain, grain)
+                outbox[j, core, :, side * grain : (side + 1) * grain, :] = jnp.where(
+                    own_left,
+                    plain_own[:, pl.ds(start, grain), side * panel : (side + 1) * panel],
+                    turned_own[:, pl.ds(deep, grain), :],
+                )
         for core in range(2):
             x_copy(j, core, pa).start()
 
     permute(0)
     pl.semaphore_wait(barrier, 5)
-    own_copy(0).start()
-    for n in range(1, BLOCKS):
-        permute(n)
-        own_copy(n).start()
+    for n in range(2):
+        own_copy(n, 0).start()
+    permute(1)
+    for n in range(2):
+        own_copy(n, 1).start()
 
     def first(j, carry):
         stage(j)
@@ -139,8 +142,11 @@
     lax.fori_loop(0, LEAD, first, 0)
     for copy in traces:
         copy.start()
-    for n in range(BLOCKS):
-        own_copy(n).wait_recv()
+    for n in range(2):
+        for c in range(2):
+            own_copy(n, c).wait_recv()
+    cross = jnp.where(own_left, 3, 2)
+    slots = ((0, cross), (5 - cross, 1))
 
     def step(j, carry):
         @pl.when(j < STEPS - LEAD)
@@ -157,31 +163,33 @@
         left = jnp.concatenate(stack, axis=0)
         size = 2 * grain
         start = pl.multiple_of(pa * quarter + j * grain, grain)
-        for n in range(width // TILE):
-            cols = slice(n * TILE, (n + 1) * TILE)
-            here = slice(n * TILE % panel, n * TILE % panel + TILE)
-            by = []
-            for c in range(2):
-                plain = mul(left, own[c, :, :, cols].reshape(width, TILE))
-                turned = mul_t(left, own[c, n * TILE // panel, here, :])
-                by.append(jnp.where(own_left, turned, plain))
-            real = (by[0][:size] - by[1][size:]).astype(jnp.bfloat16)
-            imag = (by[1][:size] + by[0][size:]).astype(jnp.bfloat16)
-            prod[0, 0, :, pl.ds(start, grain), cols] = real.reshape(2, grain, TILE)
-            prod[0, 1, :, pl.ds(start, grain), cols] = imag.reshape(2, grain, TILE)
-        y_copy(j).start()
+        for side in range(2):
+            for n in range(panel // TILE):
+                cols = slice(n * TILE, (n + 1) * TILE)
+                by = []
+                for c in range(2):
+                    top = mul(left[:, :panel], factor[slots[0][side], c, :, cols])
+                    by.append(top + mul(left[:, panel:], factor[slots[1][side], c, :, cols]))
+                real = (by[0][:size] - by[1][size:]).astype(jnp.bfloat16)
+                imag = (by[1][:size] + by[0][size:]).astype(jnp.bfloat16)
+                cols = slice(side * panel + n * TILE, side * panel + (n + 1) * TILE)
+                prod[0, 0, :, pl.ds(start, grain), cols] = real.reshape(2, grain, TILE)
+                prod[0, 1, :, pl.ds(start, grain), cols] = imag.reshape(2, grain, TILE)
+            y_copy(j, side).start()
         share(0, j).start()
 
         @pl.when(j >= LAG)
         def _():
-            y_copy(j - LAG).wait_recv()
+            for n in range(2):
+                y_copy(j - LAG, n).wait_recv()
             share(1, j - LAG).start()
 
         return carry
 
     lax.fori_loop(0, STEPS, step, 0)
     for j in range(STEPS - LAG, STEPS):
-        y_copy(j).wait_recv()
+        for n in range(2):
+            y_copy(j, n).wait_recv()
         share(1, j).start()
     load_trace.wait()
     for copy in traces:
@@ -200,26 +208,25 @@
     right_turned = jnp.where(own_second, own_left, y_left)
     within = pl.multiple_of(half * quarter + vert * rows, rows)
     whole = pl.multiple_of(pa * panel + half * quarter + vert * rows, rows)
-    unit = hot(
-        lax.broadcasted_iota(jnp.int32, (rows, rows), 0) == lax.broadcasted_iota(jnp.int32, (rows, rows), 1)
-    )
-    stack = []
+    across, down = [], []
     for c in range(2):
         plain = prod[slot_left, c, pa, pl.ds(within, rows), :]
         column = prod[slot_left, c, :, :, pl.ds(whole, rows)].reshape(width, rows)
-        turned = mul_t(unit, column).astype(jnp.bfloat16)
-        stack.append(jnp.where(left_turned, turned, plain))
-    left = jnp.concatenate(stack, axis=0)
+        across.append(jnp.where(left_turned, column.T, plain))
+        down.append(jnp.where(left_turned, column, plain.T))
+    left = jnp.concatenate(across, axis=0)
+    right = jnp.concatenate(down, axis=1)
     for n in range(width // TILE):
         cols = slice(n * TILE, (n + 1) * TILE)
         here = slice(n * TILE % panel, n * TILE % panel + TILE)
-        by = []
-        for c in range(2):
-            plain = mul(left, prod[slot_right, c, :, :, cols].reshape(width, TILE))
-            turned = mul_t(left, prod[slot_right, c, n * TILE // panel, here, :])
-            by.append(jnp.where(right_turned, turned, plain))
-        map_ref[0, :, cols] = (by[0][:rows] - by[1][rows:]).astype(jnp.bfloat16)
-        map_ref[1, :, cols] = (by[1][:rows] + by[0][rows:]).astype(jnp.bfloat16)
+        by = [mul(left, prod[slot_right, c, :, :, cols].reshape(width, TILE)) for c in range(2)]
+        to = [mul(prod[slot_right, c, n * TILE // panel, here, :], right) for c in range(2)]
+        real = (by[0][:rows] - by[1][rows:]).astype(jnp.bfloat16)
+        imag = (by[1][:rows] + by[0][rows:]).astype(jnp.bfloat16)
+        real_t = (to[0][:, :rows] - to[1][:, rows:]).astype(jnp.bfloat16)
+        imag_t = (to[1][:, :rows] + to[0][:, rows:]).astype(jnp.bfloat16)
+        map_ref[0, :, cols] = jnp.where(right_turned, real_t.T, real)
+        map_ref[1, :, cols] = jnp.where(right_turned, imag_t.T, imag)
 
     trace = (trace_all[0] + trace_all[1]) + (trace_all[2] + trace_all[3])
     wide = map_ref[...].reshape(2 * rows, width).astype(jnp.float32)
@@ -237,14 +244,16 @@
     def sent(j, carry):
         for core in range(2):
             x_copy(j, core, pa).wait_send()
-        y_copy(j).wait_send()
+        for n in range(2):
+            y_copy(j, n).wait_send()
         share(0, j).wait_send()
         share(1, j).wait_send()
         return carry
 
     lax.fori_loop(0, STEPS, sent, 0)
-    for n in range(BLOCKS):
-        own_copy(n).wait_send()
+    for n in range(2):
+        for c in range(2):
+            own_copy(n, c).wait_send()
     for copy in traces:
         copy.wait_send()
 
@@ -270,15 +279,17 @@
             pltpu.VMEM((2, panel, width), jnp.bfloat16),
             pltpu.VMEM((1, width), jnp.int32),
             pltpu.VMEM((width, width), jnp.bfloat16),
-            pltpu.VMEM((2, 2, panel, width), jnp.bfloat16),
+            pltpu.VMEM((2, panel, width), jnp.bfloat16),
+            pltpu.VMEM((2, width, panel), jnp.bfloat16),
+            pltpu.VMEM((4, 2, panel, panel), jnp.bfloat16),
             pltpu.VMEM((STEPS, 2, 2, 2 * grain, panel), jnp.bfloat16),
             pltpu.VMEM((STEPS, 2, 2, 2 * grain, panel), jnp.bfloat16),
             pltpu.VMEM((2, 2, 2, panel, width), jnp.bfloat16),
             pltpu.VMEM((4, 2, width), jnp.float32),
             dma((3,)),
-            dma((BLOCKS,)), dma((BLOCKS,)),
+            dma((2, 2)), dma((2, 2)),
             dma((STEPS, 2)), dma((STEPS, 2)),
-            dma((STEPS,)), dma((STEPS,)),
+            dma((STEPS, 2)), dma((STEPS, 2)),
             dma((2, STEPS)), dma((2, STEPS)),
             dma((4,)), dma((4,)),
         ],

time: 70.9 us -> 68.2 us (0.962)
  Pallas kernels: 68.7 us -> 66 us
    pallas_call x1, Pallas kernels: 68.7 us -> 66 us  [per_device(): pl.pallas_call(kernel, out_shape=(pltpu.VMEM((2, rows, width), jnp.bfloat...]
where the time goes in v2:
time: 68.2 us; the launch traced here: 68 us
  Pallas kernels  66 us (97%)
  local copies, waits for them, and re-layouts  1.36 us (2%)
    pallas_call x1, Pallas kernels, per_device(): pl.pallas_call(kernel, out_shape=(pltpu.VMEM((2, rows, width), jnp.bfloat...  66 us

profile of v2, /device:TPU:0, one launch (start us, length us, event | category | flops | bytes accessed | tf_op | source)
XLA Modules:
  0.0 68.0 jit_solution(7097329159120063153)
XLA Ops:
  0.6 66.0 %shard_map.68 = (bf16[2,128,1024]{2,1,0:T(8,128)(2,1)S(1)}, f32[2,128]{1,0:T(2,128)S(1)}) custom-call(s32[2,4]{1,0:T(2,128)} %bitcast.12, s32[1,4]{1,0:T(1,128)} %bitcast.13, bf16[2,512,1024]{2,1,0:T(8,128)(2,1)} %bitcast.9, s32[1,1024]{1,0:T(1,128)} %bitcast.11, f32[2,1024]{1,0:T(2,128)} %bitcast.10), custom_call_target="tpu_custom_call" | custom-call | tf_op jit(solution)/shard_map/pallas_call | solution.py:270
  66.6 0.8 %copy.9 = bf16[1,1,1,2,128,1024]{5,4,3,2,1,0:T(8,128)(2,1)} copy(bf16[1,1,1,2,128,1024]{5,4,3,2,1,0:T(8,128)(2,1)S(1)} %bitcast.7) | data formatting | bytes 1048576
  67.4 0.6 copy.10

commit v3 on v2

--- a/solution.py
+++ b/solution.py
@@ -9,6 +9,7 @@
 STEPS = 16
 LEAD = 4
 LAG = 2
+GROUP = 4
 TILE = 256
 NT = (((1,), (1,)), ((), ()))
 
@@ -76,10 +77,6 @@
             {"gx": other_x, "pa": core},
         )
 
-    def chunk(slot, j, core):
-        start = pl.multiple_of(core * quarter + j * grain, grain)
-        return prod.at[slot, :, :, pl.ds(start, grain), :]
-
     def y_copy(j, n):
         start = pl.multiple_of(pa * quarter + j * grain, grain)
         cols = slice(n * panel, (n + 1) * panel)
@@ -88,9 +85,16 @@
             ys.at[j, n], yr.at[j, n], ypeer,
         )
 
-    def share(slot, j):
-        part = chunk(slot, j, pa)
+    def share(slot, j, n):
+        start = pl.multiple_of(pa * quarter + j * grain, grain)
+        part = prod.at[slot, :, :, pl.ds(start, n * grain), :]
         return remote(part, part, ps.at[slot, j], pr.at[slot, j], cpeer)
+
+    def finish(j):
+        for core in range(2):
+            x_copy(j, core, pa).wait_send()
+        for n in range(2):
+            y_copy(j, n).wait_send()
 
     def trace_copy(n, peer):
         return remote(trace_ref, trace_all.at[n], ss.at[n], sr.at[n], peer)
@@ -114,32 +118,44 @@
             place = pl.ds(pl.multiple_of(which * panel, panel), panel)
             factor[2 * n + pa, c] = jnp.where(own_left, turned_own[c, place, :], plain_own[c, :, place])
 
-    def stage(j):
+    def lay(j, c):
         for core in range(2):
             for side in range(2):
                 start = pl.multiple_of(core * quarter + j * grain, grain)
                 deep = pl.multiple_of(side * panel + core * quarter + j * grain, grain)
-                outbox[j, core, :, side * grain : (side + 1) * grain, :] = jnp.where(
+                outbox[j, core, c, side * grain : (side + 1) * grain, :] = jnp.where(
                     own_left,
-                    plain_own[:, pl.ds(start, grain), side * panel : (side + 1) * panel],
-                    turned_own[:, pl.ds(deep, grain), :],
+                    plain_own[c, pl.ds(start, grain), side * panel : (side + 1) * panel],
+                    turned_own[c, pl.ds(deep, grain), :],
                 )
+
+    def stage(j):
+        lay(j, 0)
+        lay(j, 1)
         for core in range(2):
             x_copy(j, core, pa).start()
 
-    permute(0)
-    pl.semaphore_wait(barrier, 5)
-    for n in range(2):
-        own_copy(n, 0).start()
-    permute(1)
-    for n in range(2):
-        own_copy(n, 1).start()
+    def opening(c):
+        permute(c)
+        lay(0, c)
+        if c == 0:
+            pl.semaphore_wait(barrier, 5)
+        for core in range(2):
+            remote(
+                outbox.at[0, core, c], inbox.at[0, pa, c], xs.at[0, core], xr.at[0, pa],
+                {"gx": other_x, "pa": core},
+            ).start()
+        for n in range(2):
+            own_copy(n, c).start()
+
+    opening(0)
+    opening(1)
 
     def first(j, carry):
         stage(j)
         return carry
 
-    lax.fori_loop(0, LEAD, first, 0)
+    lax.fori_loop(1, LEAD, first, 0)
     for copy in traces:
         copy.start()
     for n in range(2):
@@ -176,31 +192,55 @@
                 prod[0, 0, :, pl.ds(start, grain), cols] = real.reshape(2, grain, TILE)
                 prod[0, 1, :, pl.ds(start, grain), cols] = imag.reshape(2, grain, TILE)
             y_copy(j, side).start()
-        share(0, j).start()
+
+        @pl.when(j % GROUP == GROUP - 1)
+        def _():
+            share(0, j + 1 - GROUP, GROUP).start()
+
+            @pl.when(j >= GROUP)
+            def _():
+                share(0, j + 1 - 2 * GROUP, GROUP).wait()
+
+        @pl.when(j >= GROUP)
+        def _():
+            finish(j - GROUP)
 
         @pl.when(j >= LAG)
         def _():
             for n in range(2):
                 y_copy(j - LAG, n).wait_recv()
-            share(1, j - LAG).start()
+
+        @pl.when((j >= LAG) & ((j - LAG) % GROUP == GROUP - 1))
+        def _():
+            share(1, j - LAG + 1 - GROUP, GROUP).start()
+
+            @pl.when(j - LAG >= GROUP)
+            def _():
+                share(1, j - LAG + 1 - 2 * GROUP, GROUP).wait()
 
         return carry
 
     lax.fori_loop(0, STEPS, step, 0)
+    rest = [share(0, STEPS - GROUP, GROUP), share(1, STEPS - 2 * GROUP, GROUP)]
+    tail = share(1, STEPS - GROUP, GROUP - LAG)
+    tail.start()
+    rest.append(tail)
     for j in range(STEPS - LAG, STEPS):
         for n in range(2):
             y_copy(j, n).wait_recv()
-        share(1, j).start()
+        tail = share(1, j, 1)
+        tail.start()
+        rest.append(tail)
+    for j in range(STEPS - GROUP, STEPS):
+        finish(j)
     load_trace.wait()
     for copy in traces:
-        copy.wait_recv()
-
-    def arrived(j, carry):
-        share(0, j).wait_recv()
-        share(1, j).wait_recv()
-        return carry
-
-    lax.fori_loop(0, STEPS, arrived, 0)
+        copy.wait()
+    for n in range(2):
+        for c in range(2):
+            own_copy(n, c).wait_send()
+    for copy in rest:
+        copy.wait()
 
     slot_left = jnp.where(own_second, 1, 0)
     slot_right = 1 - slot_left
@@ -216,6 +256,8 @@
         down.append(jnp.where(left_turned, column, plain.T))
     left = jnp.concatenate(across, axis=0)
     right = jnp.concatenate(down, axis=1)
+    trace = (trace_all[0] + trace_all[1]) + (trace_all[2] + trace_all[3])
+    folded = [[None, None], [None, None]]
     for n in range(width // TILE):
         cols = slice(n * TILE, (n + 1) * TILE)
         here = slice(n * TILE % panel, n * TILE % panel + TILE)
@@ -225,37 +267,25 @@
         imag = (by[1][:rows] + by[0][rows:]).astype(jnp.bfloat16)
         real_t = (to[0][:, :rows] - to[1][:, rows:]).astype(jnp.bfloat16)
         imag_t = (to[1][:, :rows] + to[0][:, rows:]).astype(jnp.bfloat16)
-        map_ref[0, :, cols] = jnp.where(right_turned, real_t.T, real)
-        map_ref[1, :, cols] = jnp.where(right_turned, imag_t.T, imag)
-
-    trace = (trace_all[0] + trace_all[1]) + (trace_all[2] + trace_all[3])
-    wide = map_ref[...].reshape(2 * rows, width).astype(jnp.float32)
+        for part, value in enumerate((jnp.where(right_turned, real_t.T, real), jnp.where(right_turned, imag_t.T, imag))):
+            map_ref[part, :, cols] = value
+            wide = value.astype(jnp.float32)
+            for c in range(2):
+                scaled = wide * trace[c : c + 1, cols]
+                for m in range(TILE // 128):
+                    term = scaled[:, m * 128 : (m + 1) * 128]
+                    folded[c][part] = term if folded[c][part] is None else folded[c][part] + term
+
     ones = jnp.ones((8, 128), jnp.float32)
-    sums = []
-    for c in range(2):
-        scaled = wide * trace[c : c + 1]
-        folded = scaled[:, :128]
-        for n in range(1, width // 128):
-            folded += scaled[:, n * 128 : (n + 1) * 128]
-        sums.append(lax.dot_general(ones, folded, NT, precision=lax.Precision.HIGHEST, preferred_element_type=jnp.float32))
+    sums = [
+        lax.dot_general(
+            ones, jnp.concatenate(folded[c], axis=0), NT,
+            precision=lax.Precision.HIGHEST, preferred_element_type=jnp.float32,
+        )
+        for c in range(2)
+    ]
     out_ref[0:1] = sums[0][0:1, :rows] - sums[1][0:1, rows:]
     out_ref[1:2] = sums[1][0:1, :rows] + sums[0][0:1, rows:]
-
-    def sent(j, carry):
-        for core in range(2):
-            x_copy(j, core, pa).wait_send()
-        for n in range(2):
-            y_copy(j, n).wait_send()
-        share(0, j).wait_send()
-        share(1, j).wait_send()
-        return carry
-
-    lax.fori_loop(0, STEPS, sent, 0)
-    for n in range(2):
-        for c in range(2):
-            own_copy(n, c).wait_send()
-    for copy in traces:
-        copy.wait_send()
 
 
 def per_device(leaf_maps, face_index, order_x, order_y, traces):

time: 68.2 us -> 66.9 us (0.981)
  Pallas kernels: 66 us -> 64.7 us
    pallas_call x1, Pallas kernels: 66 us -> 64.7 us  [per_device(): pl.pallas_call(kernel, out_shape=(pltpu.VMEM((2, rows, width), jnp.bfloat...]
where the time goes in v3:
time: 66.9 us; the launch traced here: 66.7 us
  Pallas kernels  64.7 us (97%)
  local copies, waits for them, and re-layouts  1.36 us (2%)
    pallas_call x1, Pallas kernels, per_device(): pl.pallas_call(kernel, out_shape=(pltpu.VMEM((2, rows, width), jnp.bfloat...  64.7 us
    unnamed x2, local copies, waits for them, and re-layouts  1.36 us

profile of v3, /device:TPU:0, one launch (start us, length us, event | category | flops | bytes accessed | tf_op | source)
XLA Modules:
  0.0 66.7 jit_solution(18401025185279021687)
XLA Ops:
  0.6 64.7 %shard_map.68 = (bf16[2,128,1024]{2,1,0:T(8,128)(2,1)S(1)}, f32[2,128]{1,0:T(2,128)S(1)}) custom-call(s32[2,4]{1,0:T(2,128)} %bitcast.12, s32[1,4]{1,0:T(1,128)} %bitcast.13, bf16[2,512,1024]{2,1,0:T(8,128)(2,1)} %bitcast.9, s32[1,1024]{1,0:T(1,128)} %bitcast.11, f32[2,1024]{1,0:T(2,128)} %bitcast.10), custom_call_target="tpu_custom_call" | custom-call | tf_op jit(solution)/shard_map/pallas_call | solution.py:300
  65.3 0.8 %copy.9 = bf16[1,1,1,2,128,1024]{5,4,3,2,1,0:T(8,128)(2,1)} copy(bf16[1,1,1,2,128,1024]{5,4,3,2,1,0:T(8,128)(2,1)S(1)} %bitcast.7) | data formatting | bytes 1048576
  66.1 0.6 copy.10

commit v4 on v3

--- a/solution.py
+++ b/solution.py
@@ -10,7 +10,7 @@
 LEAD = 4
 LAG = 2
 GROUP = 4
-TILE = 256
+TILE = 512
 NT = (((1,), (1,)), ((), ()))
 
 
@@ -77,12 +77,12 @@
             {"gx": other_x, "pa": core},
         )
 
-    def y_copy(j, n):
+    def y_copy(j, n, size=1):
         start = pl.multiple_of(pa * quarter + j * grain, grain)
-        cols = slice(n * panel, (n + 1) * panel)
+        cols = slice(n * panel, (n + size) * panel)
         return remote(
             prod.at[0, :, :, pl.ds(start, grain), cols], prod.at[1, :, :, pl.ds(start, grain), cols],
-            ys.at[j, n], yr.at[j, n], ypeer,
+            ys.at[j], yr.at[j], ypeer,
         )
 
     def share(slot, j, n):
@@ -93,8 +93,7 @@
     def finish(j):
         for core in range(2):
             x_copy(j, core, pa).wait_send()
-        for n in range(2):
-            y_copy(j, n).wait_send()
+        y_copy(j, 0, 2).wait_send()
 
     def trace_copy(n, peer):
         return remote(trace_ref, trace_all.at[n], ss.at[n], sr.at[n], peer)
@@ -114,9 +113,10 @@
             value = mul(raw[c], pick[:, cols]).astype(jnp.bfloat16)
             plain_own[c, :, cols] = value
             turned_own[c, cols, :] = value.T
-        for n, which in ((0, pa), (1, 1 - pa)):
-            place = pl.ds(pl.multiple_of(which * panel, panel), panel)
-            factor[2 * n + pa, c] = jnp.where(own_left, turned_own[c, place, :], plain_own[c, :, place])
+    def choose(n, which, c):
+        place = pl.ds(pl.multiple_of(which * panel, panel), panel)
+        factor[2 * n + pa, c] = jnp.where(own_left, turned_own[c, place, :], plain_own[c, :, place])
+        own_copy(n, c).start()
 
     def lay(j, c):
         for core in range(2):
@@ -145,8 +145,8 @@
                 outbox.at[0, core, c], inbox.at[0, pa, c], xs.at[0, core], xr.at[0, pa],
                 {"gx": other_x, "pa": core},
             ).start()
-        for n in range(2):
-            own_copy(n, c).start()
+        choose(0, pa, c)
+        choose(1, 1 - pa, c)
 
     opening(0)
     opening(1)
@@ -191,7 +191,15 @@
                 cols = slice(side * panel + n * TILE, side * panel + (n + 1) * TILE)
                 prod[0, 0, :, pl.ds(start, grain), cols] = real.reshape(2, grain, TILE)
                 prod[0, 1, :, pl.ds(start, grain), cols] = imag.reshape(2, grain, TILE)
-            y_copy(j, side).start()
+            @pl.when((j == 0) | (j == STEPS - 1))
+            def _(side=side):
+                y_copy(j, side).start()
+
+            if side:
+                @pl.when((j > 0) & (j < STEPS - 1))
+                def _():
+                    y_copy(j, 0, 2).start()
+
 
         @pl.when(j % GROUP == GROUP - 1)
         def _():
@@ -207,8 +215,7 @@
 
         @pl.when(j >= LAG)
         def _():
-            for n in range(2):
-                y_copy(j - LAG, n).wait_recv()
+            y_copy(j - LAG, 0, 2).wait_recv()
 
         @pl.when((j >= LAG) & ((j - LAG) % GROUP == GROUP - 1))
         def _():
@@ -226,8 +233,7 @@
     tail.start()
     rest.append(tail)
     for j in range(STEPS - LAG, STEPS):
-        for n in range(2):
-            y_copy(j, n).wait_recv()
+        y_copy(j, 0, 2).wait_recv()
         tail = share(1, j, 1)
         tail.start()
         rest.append(tail)
@@ -319,7 +325,7 @@
             dma((3,)),
             dma((2, 2)), dma((2, 2)),
             dma((STEPS, 2)), dma((STEPS, 2)),
-            dma((STEPS, 2)), dma((STEPS, 2)),
+            dma((STEPS,)), dma((STEPS,)),
             dma((2, STEPS)), dma((2, STEPS)),
             dma((4,)), dma((4,)),
         ],

time: 66.9 us -> 66.3 us (level)
  no operation moved by 1% of the time
where the time goes in v4:
time: 66.3 us; the launch traced here: 66.1 us
  Pallas kernels  64.1 us (97%)
  local copies, waits for them, and re-layouts  1.36 us (2%)
    pallas_call x1, Pallas kernels, per_device(): pl.pallas_call(kernel, out_shape=(pltpu.VMEM((2, rows, width), jnp.bfloat...  64.1 us
    unnamed x2, local copies, waits for them, and re-layouts  1.36 us

profile of v4, /device:TPU:0, one launch (start us, length us, event | category | flops | bytes accessed | tf_op | source)
XLA Modules:
  0.0 66.1 jit_solution(10274046363968076584)
XLA Ops:
  0.6 64.1 %shard_map.68 = (bf16[2,128,1024]{2,1,0:T(8,128)(2,1)S(1)}, f32[2,128]{1,0:T(2,128)S(1)}) custom-call(s32[2,4]{1,0:T(2,128)} %bitcast.12, s32[1,4]{1,0:T(1,128)} %bitcast.13, bf16[2,512,1024]{2,1,0:T(8,128)(2,1)} %bitcast.9, s32[1,1024]{1,0:T(1,128)} %bitcast.11, f32[2,1024]{1,0:T(2,128)} %bitcast.10), custom_call_target="tpu_custom_call" | custom-call | tf_op jit(solution)/shard_map/pallas_call | solution.py:306
  64.8 0.8 %copy.9 = bf16[1,1,1,2,128,1024]{5,4,3,2,1,0:T(8,128)(2,1)} copy(bf16[1,1,1,2,128,1024]{5,4,3,2,1,0:T(8,128)(2,1)S(1)} %bitcast.7) | data formatting | bytes 1048576
  65.6 0.6 copy.10
